TPU v7x, 32 devices: a whole 2x2x4 slice. The times are simulated.
32 devices in a mesh: band: 8 (over z, y), grid: 4 (over x, core).
Axes of the slice: x: 2, y: 2, z: 4, core: 2. Of those that a mesh axis runs over, the one named last changes fastest.
Arguments:
- orbitals: bfloat16 [16, 128, 128, 128], P('band', 'grid'), may hold values from -6 to 6
- occupation: float32 [16], replicated, may hold values from 0.25 to 2
- partner: int32 [8], replicated, may hold values from 0 to 7, as said below
- col_index: int32 [8192], replicated, may hold values from 0 to 16383, as said below
- kernel: float32 [128, 8192], P(None, 'grid'), may hold values from 0.1 to 4
Outputs:
- exchange: float32 [16, 128, 128, 128], P('band', 'grid')
Inputs may be any that keep to these rules, and one draw needn't show every extreme that they name: partner[partner[a]] = a and partner[a] != a for every block a. `col_index`: all entries are distinct; the entries at positions g * 2048 to (g + 1) * 2048 - 1 are columns of the g-th block of 4096 consecutive columns, among them that block's first and last column.
All inputs are finite; a program needn't handle non-finite values.
Results may differ from a plain program's by a relative error of at most 0.0065.
Values may be sent and summed in bfloat16 or wider, within the bound.
No kernel may reach another device: no remote copies, remote signals or barrier semaphores. Data moves between devices by JAX's collectives and lax.ppermute only.
A program may use at most 64 MiB of HBM per device.

v0:
```python
import math
import jax
import jax.numpy as jnp
import numpy as np
from jax import lax
from jax.sharding import PartitionSpec as P

NX = 128
NY = 128
NZ = 128


def tables(length):
    counter = jnp.arange(length, dtype=jnp.int32)
    product = counter[:, None] * counter[None, :] % length
    angles = product.astype(jnp.float32) * (2.0 * math.pi / length)
    return (jnp.cos(angles).astype(jnp.bfloat16), jnp.sin(angles).astype(jnp.bfloat16))


def contract(pattern, left_side, right_side):
    return jnp.einsum(pattern, left_side, right_side, preferred_element_type=jnp.float32)


def fetch_block(block_data, partner):
    band_count = lax.axis_size("band")
    spread = lax.all_to_all(block_data, "band", split_axis=2, concat_axis=2, tiled=True)
    dims = spread.shape
    pieces = spread.reshape(dims[0], dims[1], band_count, dims[2] // band_count, dims[3])
    pieces = jnp.take(pieces, partner, axis=2).reshape(dims)
    return lax.all_to_all(pieces, "band", split_axis=2, concat_axis=2, tiled=True)


def return_block(block_data, partner):
    band_count = lax.axis_size("band")
    spread = lax.all_to_all(
        block_data.astype(jnp.bfloat16), "band", split_axis=2, concat_axis=2, tiled=True
    ).astype(block_data.dtype)
    dims = spread.shape
    pieces = spread.reshape(dims[0], dims[1], band_count, dims[2] // band_count, dims[3])
    pieces = jnp.take(pieces, partner, axis=2).reshape(dims)
    return lax.all_to_all(
        pieces.astype(jnp.bfloat16), "band", split_axis=2, concat_axis=2, tiled=True
    ).astype(pieces.dtype)


def local(orbitals, occupation, partner, col_index, kernel):
    block_bands = orbitals.shape[0]
    slab_rows = orbitals.shape[1]
    half_block = block_bands // 2
    pair_count = block_bands * half_block
    band_pos = lax.axis_index("band")
    partner_block = partner[band_pos]
    theirs = fetch_block(orbitals, partner)
    parity = (band_pos > partner_block).astype(jnp.int32)
    slot_table = np.arange(pair_count)
    left_table = slot_table // half_block
    left_index = jnp.asarray(left_table, jnp.int32)
    right_index = (left_index + parity) % 2 + 2 * jnp.asarray(slot_table % half_block, jnp.int32)
    left_bands = orbitals[left_table]
    right_bands = jnp.take(theirs, right_index, axis=0)
    density = (left_bands.astype(jnp.float32) * right_bands.astype(jnp.float32)).astype(
        jnp.bfloat16
    )
    xcosine, xsines = tables(NX)
    ycosine, ysines = tables(NY)
    zcosine, zsines = tables(NZ)
    ztable = jnp.concatenate([zcosine, -zsines], axis=1)
    first_both = contract("pxyz,zk->pxyk", density, ztable).astype(jnp.bfloat16)
    first_real = first_both[..., :NZ]
    first_imag = first_both[..., NZ:]
    second_real = (
        contract("pxyk,yq->pxqk", first_real, ycosine)
        + contract("pxyk,yq->pxqk", first_imag, ysines)
    ).astype(jnp.bfloat16)
    second_imag = (
        contract("pxyk,yq->pxqk", first_imag, ycosine)
        - contract("pxyk,yq->pxqk", first_real, ysines)
    ).astype(jnp.bfloat16)
    second_real = second_real.reshape(pair_count, slab_rows, NY * NZ)
    second_imag = second_imag.reshape(pair_count, slab_rows, NY * NZ)
    norm_scale = 1.0 / (NX * NY * NZ)
    grid_pos = lax.axis_index("grid")
    column_count = kernel.shape[1]
    column_span = NY * NZ // lax.axis_size("grid")
    local_cols = (
        lax.dynamic_slice_in_dim(col_index, grid_pos * column_count, column_count, 0)
        - grid_pos * column_span
    )
    kern_local = (
        jnp.zeros((NX, column_span), jnp.float32).at[:, local_cols].set(kernel * norm_scale)
    )
    column_real = lax.all_to_all(second_real, "grid", split_axis=2, concat_axis=1, tiled=True)
    column_imag = lax.all_to_all(second_imag, "grid", split_axis=2, concat_axis=1, tiled=True)
    scaled_real = contract("pxc,xk->pkc", column_real, xcosine) + contract(
        "pxc,xk->pkc", column_imag, xsines
    )
    scaled_imag = contract("pxc,xk->pkc", column_imag, xcosine) - contract(
        "pxc,xk->pkc", column_real, xsines
    )
    scaled_real = (scaled_real * kern_local).astype(jnp.bfloat16)
    scaled_imag = (scaled_imag * kern_local).astype(jnp.bfloat16)
    third_real = (
        contract("pkc,xk->pxc", scaled_real, xcosine) - contract("pkc,xk->pxc", scaled_imag, xsines)
    ).astype(jnp.bfloat16)
    third_imag = (
        contract("pkc,xk->pxc", scaled_imag, xcosine) + contract("pkc,xk->pxc", scaled_real, xsines)
    ).astype(jnp.bfloat16)
    back_real = lax.all_to_all(third_real, "grid", split_axis=1, concat_axis=2, tiled=True)
    back_imag = lax.all_to_all(third_imag, "grid", split_axis=1, concat_axis=2, tiled=True)
    back_real = back_real.reshape(pair_count, slab_rows, NY, NZ)
    back_imag = back_imag.reshape(pair_count, slab_rows, NY, NZ)
    fourth_real = (
        contract("pxqk,yq->pxyk", back_real, ycosine) - contract("pxqk,yq->pxyk", back_imag, ysines)
    ).astype(jnp.bfloat16)
    fourth_imag = (
        contract("pxqk,yq->pxyk", back_imag, ycosine) + contract("pxqk,yq->pxyk", back_real, ysines)
    ).astype(jnp.bfloat16)
    fourth_both = jnp.concatenate([fourth_real, fourth_imag], axis=3)
    potential = contract("pxyk,zk->pxyz", fourth_both, ztable)
    own_occ = lax.dynamic_slice_in_dim(occupation, band_pos * block_bands, block_bands, 0)
    their_occ = lax.dynamic_slice_in_dim(occupation, partner_block * block_bands, block_bands, 0)
    right_weight = jnp.take(their_occ, right_index)
    left_weight = jnp.take(own_occ, left_index)
    own_terms = potential * right_weight[:, None, None, None] * right_bands.astype(jnp.float32)
    their_terms = potential * left_weight[:, None, None, None] * left_bands.astype(jnp.float32)
    own_sum = jnp.sum(own_terms.reshape((block_bands, half_block) + own_terms.shape[1:]), axis=1)
    their_sum = jnp.stack(
        [
            jnp.sum(
                jnp.where((right_index == band_number)[:, None, None, None], their_terms, 0.0),
                axis=0,
            )
            for band_number in range(block_bands)
        ]
    )
    returned = return_block(their_sum, partner)
    return -(own_sum + returned)


def solution(mesh):
    in_specs = (P("band", "grid", None, None), P(), P(), P(), P(None, "grid"))
    out_specs = P("band", "grid", None, None)
    return jax.shard_map(local, mesh=mesh, in_specs=in_specs, out_specs=out_specs, check_vma=False)
```

profile of v0, /device:TPU:0, one launch (start us, length us, event | category | flops | bytes accessed | tf_op | source)
XLA Modules:
  0.0 473.9 jit_solution(9699530073143437805)
XLA Ops:
  0.0 4.3 copy.101
  4.3 7.4 %all-to-all-start = ((bf16[2,32,128,128]{3,1,0,2:T(8,128)(2,1)}), bf16[2,32,128,128]{3,1,0,2:T(8,128)(2,1)S(1)}, u32[]{:S(2)}, u32[]{:S(2)}) async-start(bf16[2,32,128,128]{3,1,0,2:T(8,128)(2,1)} %copy.101), calls=%async_computation | async-start | bytes 4194304 | tf_op jit(solution)/shard_map/all_to_all | solution.py:26
  11.9 48.0 %all-to-all-done = bf16[2,32,128,128]{3,1,0,2:T(8,128)(2,1)S(1)} async-done(((bf16[2,32,128,128]{3,1,0,2:T(8,128)(2,1)}), bf16[2,32,128,128]{3,1,0,2:T(8,128)(2,1)S(1)}, u32[]{:S(2)}, u32[]{:S(2)}) %all-to-all-start) | async-done | bytes 2097184 | tf_op jit(solution)/shard_map/all_to_all | solution.py:26
  59.9 2.7 copy.102
  62.6 2.7 gather_fusion.1
  66.2 2.7 copy.104
  68.9 5.0 %all-to-all-start.1 = ((bf16[2,32,128,128]{3,1,0,2:T(8,128)(2,1)}), bf16[2,32,128,128]{3,1,0,2:T(8,128)(2,1)}, u32[]{:S(2)}, u32[]{:S(2)}) async-start(bf16[2,32,128,128]{3,1,0,2:T(8,128)(2,1)} %copy.104), calls=%async_computation.1 | async-start | bytes 4194304 | tf_op jit(solution)/shard_map/all_to_all | solution.py:30
  74.0 2.2 gather_fusion
  77.9 43.8 %all-to-all-done.1 = bf16[2,32,128,128]{3,1,0,2:T(8,128)(2,1)} async-done(((bf16[2,32,128,128]{3,1,0,2:T(8,128)(2,1)}), bf16[2,32,128,128]{3,1,0,2:T(8,128)(2,1)}, u32[]{:S(2)}, u32[]{:S(2)}) %all-to-all-start.1) | async-done | bytes 2097184 | tf_op jit(solution)/shard_map/all_to_all | solution.py:30
  121.8 4.3 copy.105
  126.0 2.5 gather_fusion.2
  128.6 3.7 convolution_convert_fusion
  132.3 1.0 fusion.19
  133.2 1.0 copy-done
  134.3 1.0 fusion.28
  135.2 9.4 %copy.157 = bf16[2,32,128,128]{1,0,3,2:T(2,128)(2,1)} copy(bf16[2,32,128,128]{3,2,1,0:T(8,128)(2,1)S(1)} %fusion.28) | data formatting | bytes 4194304 | tf_op jit(solution)/shard_map/reshape | solution.py:80
  144.6 10.5 %reshape.144 = bf16[4,2,131072]{2,1,0:T(2,128)(2,1)} reshape(bf16[16384,2,32]{2,1,0:T(2,128)(2,1)} %bitcast.125) | data formatting | bytes 4194304
  155.1 3.8 all-to-all-start.3
  158.9 2.7 fusion.23
  161.7 2.3 fusion.25
  164.0 13.7 %copy.153 = bf16[2,32,128,128]{1,0,3,2:T(2,128)(2,1)} copy(bf16[2,32,128,128]{3,2,1,0:T(8,128)(2,1)} %fusion.25) | data formatting | bytes 4194304 | tf_op jit(solution)/shard_map/reshape | solution.py:79
  177.7 10.6 %reshape.146 = bf16[4,2,131072]{2,1,0:T(2,128)(2,1)} reshape(bf16[16384,2,32]{2,1,0:T(2,128)(2,1)} %bitcast.126) | data formatting | bytes 4194304
  188.3 4.5 all-to-all-start.2
  192.7 1.3 multiply_bitcast_fusion
  194.1 1.3 copy.116
  196.1 7.5 %scatter_custom_fusion = f32[128,4096]{0,1:T(8,128)} fusion(s32[2048]{0:T(1024)S(1)} %compare_select_fusion, f32[2048,128]{1,0:T(8,128)} %copy.116, f32[]{:T(128)} %constant.128.clone.1), kind=kCustom, calls=%fused_computation.58 | custom fusion | bytes 2097664 | tf_op jit(solution)/shard_map/scatter | solution.py:90
  203.6 2.9 copy.117
  206.6 5.6 %reshape.145 = bf16[16384,2,32]{2,1,0:T(2,128)(2,1)} reshape(bf16[4,2,131072]{2,1,0:T(2,128)(2,1)S(1)} %all-to-all-done.3) | data formatting | bytes 4194304
  212.2 16.7 %copy.114 = bf16[2,32,4,4096]{3,1,2,0:T(8,128)(2,1)S(1)} copy(bf16[2,32,4,4096]{1,0,3,2:T(2,128)(2,1)} %bitcast.127) | data formatting | bytes 4194304 | tf_op jit(solution)/shard_map/all_to_all | solution.py:93
  228.9 3.0 fusion.55
  231.9 7.4 %reshape.147 = bf16[16384,2,32]{2,1,0:T(2,128)(2,1)} reshape(bf16[4,2,131072]{2,1,0:T(2,128)(2,1)} %all-to-all-done.2) | data formatting | bytes 4194304
  239.3 18.0 %copy.109 = bf16[2,32,4,4096]{3,1,2,0:T(8,128)(2,1)} copy(bf16[2,32,4,4096]{1,0,3,2:T(2,128)(2,1)} %bitcast.128) | data formatting | bytes 4194304 | tf_op jit(solution)/shard_map/all_to_all | solution.py:92
  257.4 2.7 fusion.57
  260.2 3.2 fusion.8
  263.4 0.9 fusion.59
  264.7 1.0 fusion.9
  265.7 1.3 copy-done.8
  267.1 0.9 fusion.6
  268.0 3.5 copy.123
  271.5 4.6 all-to-all-start.5
  276.1 0.9 fusion.61
  277.7 0.9 fusion.7
  278.6 3.5 copy.120
  282.2 19.6 %all-to-all-done.5 = bf16[2,128,4096]{2,0,1:T(2,128)(2,1)} async-done(((bf16[2,128,4096]{2,0,1:T(2,128)(2,1)}), bf16[2,128,4096]{2,0,1:T(2,128)(2,1)}, u32[]{:S(2)}, u32[]{:S(2)}) %all-to-all-start.5) | async-done | bytes 2097184 | tf_op jit(solution)/shard_map/all_to_all | solution.py:109
  301.8 4.8 %all-to-all-start.4 = ((bf16[2,128,4096]{2,0,1:T(2,128)(2,1)}), bf16[2,128,4096]{2,0,1:T(2,128)(2,1)}, u32[]{:S(2)}, u32[]{:S(2)}) async-start(bf16[2,128,4096]{2,0,1:T(2,128)(2,1)} %copy.120), calls=%async_computation.4 | async-start | bytes 4194304 | tf_op jit(solution)/shard_map/all_to_all | solution.py:108
  308.1 4.8 %copy.163 = bf16[2,4,32,4096]{3,1,2,0:T(4,128)(2,1)} copy(bf16[2,4,32,4096]{3,0,2,1:T(2,128)(2,1)} %bitcast.39) | data formatting | bytes 4194304 | tf_op jit(solution)/shard_map/all_to_all | solution.py:109
  312.9 3.8 reshape.63
  316.7 3.1 fusion.43
  319.8 12.6 %all-to-all-done.4 = bf16[2,128,4096]{2,0,1:T(2,128)(2,1)} async-done(((bf16[2,128,4096]{2,0,1:T(2,128)(2,1)}), bf16[2,128,4096]{2,0,1:T(2,128)(2,1)}, u32[]{:S(2)}, u32[]{:S(2)}) %all-to-all-start.4) | async-done | bytes 2097184 | tf_op jit(solution)/shard_map/all_to_all | solution.py:108
  332.4 4.8 %copy.164 = bf16[2,4,32,4096]{3,1,2,0:T(4,128)(2,1)} copy(bf16[2,4,32,4096]{3,0,2,1:T(2,128)(2,1)} %bitcast.34) | data formatting | bytes 4194304 | tf_op jit(solution)/shard_map/all_to_all | solution.py:108
  337.2 4.8 %reshape.62 = bf16[2,32,128,128]{3,2,1,0:T(8,128)(2,1)} reshape(bf16[2,32,4,4096]{3,2,1,0:T(4,128)(2,1)} %bitcast.138) | data formatting | bytes 4194304 | tf_op jit(solution)/shard_map/reshape | solution.py:110
  342.0 2.9 fusion.45
  345.5 1.1 fusion.32
  346.6 1.2 fusion.31
  348.2 4.8 %select_reduce_fusion.1 = (bf16[32,128,128]{2,1,0:T(8,128)(2,1)S(1)}, bf16[32,128,128]{2,1,0:T(8,128)(2,1)S(1)}, f32[2,32,128,128]{3,2,1,0:T(8,128)}) fusion(bf16[2,32,128,128]{3,2,1,0:T(8,128)(2,1)S(1)} %copy-done.12, f32[2]{0:T(128)S(1)} %compare_select_fusion.5, pred[2]{0:T(512)(128)(4,1)S(1)} %get-tuple-element.11, ...), kind=kOutput, calls=%fused_computation.34 | convolution fusion | flops 551682048 | bytes 12648460 | tf_op jit(solution)/shard_map/pxyk,zk->pxyz/dot_general | solution.py:21
  353.2 1.4 copy.129
  354.6 51.4 %all_to_all.86 = bf16[2,32,128,128]{3,1,0,2:T(8,128)(2,1)S(1)} all-to-all(bf16[2,32,128,128]{3,1,0,2:T(8,128)(2,1)S(1)} %copy.129), channel_id=1, replica_groups=mesh['band'=8,'grid'=4] {'band'}, dimensions={2} | all-to-all | bytes 4194304 | tf_op jit(solution)/shard_map/all_to_all | solution.py:35
  406.0 1.4 copy.130
  407.3 2.3 gather_fusion.5
  409.6 2.2 copy.131
  412.6 2.7 copy.132
  415.2 4.5 all-to-all-start.7
  420.4 46.7 %all-to-all-done.7 = bf16[2,32,128,128]{3,1,0,2:T(8,128)(2,1)} async-done(((bf16[2,32,128,128]{3,1,0,2:T(8,128)(2,1)}), bf16[2,32,128,128]{3,1,0,2:T(8,128)(2,1)}, u32[]{:S(2)}, u32[]{:S(2)}) %all-to-all-start.7) | async-done | bytes 2097184 | tf_op jit(solution)/shard_map/all_to_all | solution.py:41
  467.0 6.7 %fusion.12 = f32[2,32,128,128]{3,2,1,0:T(8,128)} fusion(f32[2,32,128,128]{3,2,1,0:T(8,128)} %get-tuple-element.9, bf16[2,32,128,128]{3,1,0,2:T(8,128)(2,1)} %all-to-all-done.7, f32[2]{0:T(128)S(1)} %broadcast_select_fusion.2, bf16[2,32,128,128]{3,2,1,0:T(8,128)(2,1)S(1)} %copy-done.4, pred[2]{0:T(512)(128)(4,1)S(1)} %compare_and_fusion.1), kind=kLoop, calls=%fused_computation.26 | loop fusion | flops 7340032 | bytes 12582922 | tf_op jit(solution)/shard_map/neg | solution.py:137
  (56 shorter events, 7.6 us)
Async XLA Ops:
  4.3 7.4 %copy-start.15 = (s32[8]{0:T(128)S(1)}, s32[8]{0:T(128)}, u32[]{:S(2)}) copy-start(s32[8]{0:T(128)} %param.11) | copy-start | bytes 100
  4.3 55.7 %all-to-all-start = ((bf16[2,32,128,128]{3,1,0,2:T(8,128)(2,1)}), bf16[2,32,128,128]{3,1,0,2:T(8,128)(2,1)S(1)}, u32[]{:S(2)}, u32[]{:S(2)}) async-start(bf16[2,32,128,128]{3,1,0,2:T(8,128)(2,1)} %copy.101), calls=%async_computation | async-start | bytes 4194304 | tf_op jit(solution)/shard_map/all_to_all | solution.py:26
  68.9 5.0 %copy-start.13 = (bf16[2,32,128,128]{3,2,1,0:T(8,128)(2,1)S(1)}, bf16[2,32,128,128]{3,2,1,0:T(8,128)(2,1)}, u32[]{:S(2)}) copy-start(bf16[2,32,128,128]{3,2,1,0:T(8,128)(2,1)} %param.9) | copy-start | bytes 6291460
  68.9 52.8 %all-to-all-start.1 = ((bf16[2,32,128,128]{3,1,0,2:T(8,128)(2,1)}), bf16[2,32,128,128]{3,1,0,2:T(8,128)(2,1)}, u32[]{:S(2)}, u32[]{:S(2)}) async-start(bf16[2,32,128,128]{3,1,0,2:T(8,128)(2,1)} %copy.104), calls=%async_computation.1 | async-start | bytes 4194304 | tf_op jit(solution)/shard_map/all_to_all | solution.py:30
  128.6 3.7 copy-start.3
  132.2 2.0 copy-start
  155.1 33.1 %all-to-all-start.3 = ((bf16[4,2,131072]{2,1,0:T(2,128)(2,1)}), bf16[4,2,131072]{2,1,0:T(2,128)(2,1)S(1)}, u32[]{:S(2)}, u32[]{:S(2)}) async-start(bf16[4,2,131072]{2,1,0:T(2,128)(2,1)} %reshape.144), calls=%async_computation.3 | async-start | bytes 4194304 | tf_op jit(solution)/shard_map/all_to_all | solution.py:93
  158.9 2.8 copy-start.1
  188.3 43.6 %all-to-all-start.2 = ((bf16[4,2,131072]{2,1,0:T(2,128)(2,1)}), bf16[4,2,131072]{2,1,0:T(2,128)(2,1)}, u32[]{:S(2)}, u32[]{:S(2)}) async-start(bf16[4,2,131072]{2,1,0:T(2,128)(2,1)} %reshape.146), calls=%async_computation.2 | async-start | bytes 4194304 | tf_op jit(solution)/shard_map/all_to_all | solution.py:92
  257.4 2.7 copy-start.2
  257.4 2.9 copy-start.5
  263.4 1.3 copy-start.6
  265.7 1.3 copy-start.8
  271.5 4.6 copy-start.9
  271.5 30.3 %all-to-all-start.5 = ((bf16[2,128,4096]{2,0,1:T(2,128)(2,1)}), bf16[2,128,4096]{2,0,1:T(2,128)(2,1)}, u32[]{:S(2)}, u32[]{:S(2)}) async-start(bf16[2,128,4096]{2,0,1:T(2,128)(2,1)} %copy.123), calls=%async_computation.5 | async-start | bytes 4194304 | tf_op jit(solution)/shard_map/all_to_all | solution.py:109
  276.1 1.6 copy-start.7
  282.2 25.1 %copy-start.14 = (f32[16]{0:T(128)S(1)}, f32[16]{0:T(128)}, u32[]{:S(2)}) copy-start(f32[16]{0:T(128)} %param.10) | copy-start | bytes 196
  301.8 30.6 %all-to-all-start.4 = ((bf16[2,128,4096]{2,0,1:T(2,128)(2,1)}), bf16[2,128,4096]{2,0,1:T(2,128)(2,1)}, u32[]{:S(2)}, u32[]{:S(2)}) async-start(bf16[2,128,4096]{2,0,1:T(2,128)(2,1)} %copy.120), calls=%async_computation.4 | async-start | bytes 4194304 | tf_op jit(solution)/shard_map/all_to_all | solution.py:108
  342.0 2.9 copy-start.10
  342.0 3.5 copy-start.11
  346.6 1.6 copy-start.12
  415.2 51.8 %copy-start.4 = (bf16[2,32,128,128]{3,2,1,0:T(8,128)(2,1)S(1)}, bf16[2,32,128,128]{3,2,1,0:T(8,128)(2,1)}, u32[]{:S(2)}) copy-start(bf16[2,32,128,128]{3,2,1,0:T(8,128)(2,1)} %copy-done.3) | copy-start | bytes 6291460
  415.2 51.8 %all-to-all-start.7 = ((bf16[2,32,128,128]{3,1,0,2:T(8,128)(2,1)}), bf16[2,32,128,128]{3,1,0,2:T(8,128)(2,1)}, u32[]{:S(2)}, u32[]{:S(2)}) async-start(bf16[2,32,128,128]{3,1,0,2:T(8,128)(2,1)} %copy.132), calls=%async_computation.7 | async-start | bytes 4194304 | tf_op jit(solution)/shard_map/all_to_all | solution.py:41
where the time goes:
time: 481 us; the launch traced here: 474 us
  waiting for transfers between devices  171 us (36%)
  local copies, waits for them, and re-layouts  167 us (35%)
  blocking collectives  51.4 us (11%)
  matrix products  37.3 us (8%)
  starting transfers between devices  34.6 us (7%)
  other arithmetic  10.5 us (2%)
    all_to_all x1, blocking collectives, return_block(): lax.all_to_all(block_data.astype(jnp.bfloat16), 'band', split_axis=2, con...  51.4 us
    all_to_all x1, waiting for transfers between devices, fetch_block(): lax.all_to_all(block_data, 'band', split_axis=2, concat_axis=2, tiled=True)  48 us
    all_to_all x1, waiting for transfers between devices, return_block(): lax.all_to_all(pieces.astype(jnp.bfloat16), 'band', split_axis=2, concat_...  46.7 us
    all_to_all x1, waiting for transfers between devices, fetch_block(): lax.all_to_all(pieces, 'band', split_axis=2, concat_axis=2, tiled=True)  43.8 us
    unnamed x37, local copies, waits for them, and re-layouts  43.1 us
    dot_general x18, matrix products, contract(): jnp.einsum(pattern, left_side, right_side, preferred_element_type=jnp.flo...  37.3 us
    all_to_all x1, waiting for transfers between devices, local(): lax.all_to_all(third_imag, 'grid', split_axis=1, concat_axis=2, tiled=True)  19.6 us
    all_to_all x1, local copies, waits for them, and re-layouts, local(): lax.all_to_all(second_real, 'grid', split_axis=2, concat_axis=1, tiled=True)  18 us
  transfers between devices with their start and end apart: 7, of which 5 were waited for; matrix products, arithmetic and copies ran while one was open for 19% of the time, Pallas kernels for 0%

commit v1 on v0

--- a/solution.py
+++ b/solution.py
@@ -8,6 +8,18 @@
 NX = 128
 NY = 128
 NZ = 128
+
+
+def exchange_directly(x, axis, split, join):
+    ways, here = (lax.axis_size(axis), lax.axis_index(axis))
+    width = x.shape[split] // ways
+    turned = jnp.roll(x, -here * width, axis=split)
+    got = [lax.slice_in_dim(turned, 0, width, axis=split)]
+    for far in range(1, ways):
+        sent = lax.slice_in_dim(turned, far * width, (far + 1) * width, axis=split)
+        got.append(lax.ppermute(sent, axis, [(d, (d + far) % ways) for d in range(ways)]))
+    line = jnp.concatenate(got[::-1], axis=join)
+    return jnp.roll(line, (here + 1) * got[0].shape[join], axis=join)
 
 
 def tables(length):
@@ -23,7 +35,7 @@
 
 def fetch_block(block_data, partner):
     band_count = lax.axis_size("band")
-    spread = lax.all_to_all(block_data, "band", split_axis=2, concat_axis=2, tiled=True)
+    spread = exchange_directly(block_data, "band", 2, 2)
     dims = spread.shape
     pieces = spread.reshape(dims[0], dims[1], band_count, dims[2] // band_count, dims[3])
     pieces = jnp.take(pieces, partner, axis=2).reshape(dims)

time: 481 us -> 478 us (level)
  waiting for transfers between devices: 171 us -> 161 us
    all_to_all x1 -> x0, waiting for transfers between devices: 48 us -> none  [fetch_block(): lax.all_to_all(block_data, 'band', split_axis=2, concat_axis=2, tiled=True)]
    ppermute x0 -> x7, waiting for transfers between devices: none -> 38.4 us  [exchange_directly(): lax.ppermute(sent, axis, [(d, (d + far) % ways) for d in range(ways)])]
    ppermute x0 -> x7, starting transfers between devices: none -> 9.47 us  [exchange_directly(): lax.ppermute(sent, axis, [(d, (d + far) % ways) for d in range(ways)])]
    all_to_all x1 -> x0, starting transfers between devices: 7.44 us -> none  [fetch_block(): lax.all_to_all(block_data, 'band', split_axis=2, concat_axis=2, tiled=True)]
    unnamed x37 -> x43, local copies, waits for them, and re-layouts: 43.1 us -> 43.9 us
  transfers between devices with their start and end apart: 7 -> 13, of which waited for: 5 -> 8; matrix products, arithmetic and copies ran while one was open for 19% -> 20% of each run, Pallas kernels for 0% -> 0%
where the time goes in v1:
time: 478 us; the launch traced here: 471 us
  local copies, waits for them, and re-layouts  168 us (35%)
  waiting for transfers between devices  161 us (34%)
  blocking collectives  51.4 us (11%)
  matrix products  37.3 us (8%)
  starting transfers between devices  36.6 us (8%)
  other arithmetic  14.1 us (3%)
    all_to_all x1, blocking collectives, return_block(): lax.all_to_all(block_data.astype(jnp.bfloat16), 'band', split_axis=2, con...  51.4 us
    all_to_all x1, waiting for transfers between devices, return_block(): lax.all_to_all(pieces.astype(jnp.bfloat16), 'band', split_axis=2, concat_...  46.7 us
    unnamed x43, local copies, waits for them, and re-layouts  43.9 us
    all_to_all x1, waiting for transfers between devices, fetch_block(): lax.all_to_all(pieces, 'band', split_axis=2, concat_axis=2, tiled=True)  43.7 us
    ppermute x7, waiting for transfers between devices, exchange_directly(): lax.ppermute(sent, axis, [(d, (d + far) % ways) for d in range(ways)])  38.4 us
    dot_general x18, matrix products, contract(): jnp.einsum(pattern, left_side, right_side, preferred_element_type=jnp.flo...  37.3 us
    all_to_all x1, waiting for transfers between devices, local(): lax.all_to_all(third_imag, 'grid', split_axis=1, concat_axis=2, tiled=True)  19.6 us
    all_to_all x1, local copies, waits for them, and re-layouts, local(): lax.all_to_all(second_real, 'grid', split_axis=2, concat_axis=1, tiled=True)  18 us
  transfers between devices with their start and end apart: 13, of which 8 were waited for; matrix products, arithmetic and copies ran while one was open for 20% of the time, Pallas kernels for 0%

profile of v1, /device:TPU:0, one launch (start us, length us, event | category | flops | bytes accessed | tf_op | source)
XLA Modules:
  0.0 470.8 jit_solution(2341656597642316837)
XLA Ops:
  0.0 2.5 fusion.19
  2.5 1.2 fusion.134
  3.7 6.0 %collective-permute-start = (bf16[2,32,16,128]{3,2,1,0:T(8,128)(2,1)}, bf16[2,32,16,128]{3,2,1,0:T(8,128)(2,1)}, u32[]{:S(2)}, u32[]{:S(2)}) collective-permute-start(bf16[2,32,16,128]{3,2,1,0:T(8,128)(2,1)} %get-tuple-element.14), channel_id=1, source_target_pairs={{0,28},{4,0},{8,4},{12,8},{16,12},{20,16},{24,20},{28,24},{1,29},{... | collective-permute-start | bytes 786440 | tf_op jit(solution)/shard_map/ppermute | solution.py:20
  10.2 3.0 collective-permute-start.3
  13.4 3.5 collective-permute-done
  17.8 4.6 collective-permute-done.1
  23.4 4.6 collective-permute-done.2
  29.0 25.8 %collective-permute-done.3 = bf16[2,32,16,128]{3,2,1,0:T(8,128)(2,1)} collective-permute-done((bf16[2,32,16,128]{3,2,1,0:T(8,128)(2,1)S(1)}, bf16[2,32,16,128]{3,2,1,0:T(8,128)(2,1)}, u32[]{:S(2)}, u32[]{:S(2)}) %collective-permute-start.3) | collective-permute-done | bytes 262176 | tf_op jit(solution)/shard_map/ppermute | solution.py:20
  55.8 1.0 constant_dynamic-update-slice_fusion.2
  57.0 1.1 fusion.18
  58.1 2.3 gather_fusion.1
  60.3 2.2 copy.97
  62.9 2.7 copy.98
  65.6 5.0 %all-to-all-start = ((bf16[2,32,128,128]{3,1,0,2:T(8,128)(2,1)}), bf16[2,32,128,128]{3,1,0,2:T(8,128)(2,1)}, u32[]{:S(2)}, u32[]{:S(2)}) async-start(bf16[2,32,128,128]{3,1,0,2:T(8,128)(2,1)} %copy.98), calls=%async_computation | async-start | bytes 4194304 | tf_op jit(solution)/shard_map/all_to_all | solution.py:42
  71.8 2.2 gather_fusion
  74.6 43.7 %all-to-all-done = bf16[2,32,128,128]{3,1,0,2:T(8,128)(2,1)} async-done(((bf16[2,32,128,128]{3,1,0,2:T(8,128)(2,1)}), bf16[2,32,128,128]{3,1,0,2:T(8,128)(2,1)}, u32[]{:S(2)}, u32[]{:S(2)}) %all-to-all-start) | async-done | bytes 2097184 | tf_op jit(solution)/shard_map/all_to_all | solution.py:42
  118.3 4.3 copy.99
  122.5 2.5 gather_fusion.2
  125.1 3.7 convolution_convert_fusion
  129.7 1.0 copy-done
  131.7 9.4 %copy.151 = bf16[2,32,128,128]{1,0,3,2:T(2,128)(2,1)} copy(bf16[2,32,128,128]{3,2,1,0:T(8,128)(2,1)S(1)} %fusion.30) | data formatting | bytes 4194304 | tf_op jit(solution)/shard_map/reshape | solution.py:92
  141.2 10.5 %reshape.144 = bf16[4,2,131072]{2,1,0:T(2,128)(2,1)} reshape(bf16[16384,2,32]{2,1,0:T(2,128)(2,1)} %bitcast.125) | data formatting | bytes 4194304
  151.7 3.8 all-to-all-start.2
  155.5 2.7 fusion.25
  158.3 2.3 fusion.27
  160.6 13.8 %copy.147 = bf16[2,32,128,128]{1,0,3,2:T(2,128)(2,1)} copy(bf16[2,32,128,128]{3,2,1,0:T(8,128)(2,1)} %fusion.27) | data formatting | bytes 4194304 | tf_op jit(solution)/shard_map/reshape | solution.py:91
  174.4 10.6 %reshape.146 = bf16[4,2,131072]{2,1,0:T(2,128)(2,1)} reshape(bf16[16384,2,32]{2,1,0:T(2,128)(2,1)} %bitcast.126) | data formatting | bytes 4194304
  185.0 4.5 all-to-all-start.1
  189.4 1.3 multiply_bitcast_fusion
  190.7 1.3 copy.110
  192.8 7.5 %scatter_custom_fusion = f32[128,4096]{0,1:T(8,128)} fusion(s32[2048]{0:T(1024)S(1)} %compare_select_fusion, f32[2048,128]{1,0:T(8,128)} %copy.110, f32[]{:T(128)} %constant.147.clone.1), kind=kCustom, calls=%fused_computation.64 | custom fusion | bytes 2097664 | tf_op jit(solution)/shard_map/scatter | solution.py:102
  200.3 2.9 copy.111
  203.3 5.6 %reshape.145 = bf16[16384,2,32]{2,1,0:T(2,128)(2,1)} reshape(bf16[4,2,131072]{2,1,0:T(2,128)(2,1)S(1)} %all-to-all-done.2) | data formatting | bytes 4194304
  208.9 16.7 %copy.108 = bf16[2,32,4,4096]{3,1,2,0:T(8,128)(2,1)S(1)} copy(bf16[2,32,4,4096]{1,0,3,2:T(2,128)(2,1)} %bitcast.127) | data formatting | bytes 4194304 | tf_op jit(solution)/shard_map/all_to_all | solution.py:105
  225.6 3.0 fusion.57
  228.6 7.4 %reshape.147 = bf16[16384,2,32]{2,1,0:T(2,128)(2,1)} reshape(bf16[4,2,131072]{2,1,0:T(2,128)(2,1)} %all-to-all-done.1) | data formatting | bytes 4194304
  236.1 18.0 %copy.103 = bf16[2,32,4,4096]{3,1,2,0:T(8,128)(2,1)} copy(bf16[2,32,4,4096]{1,0,3,2:T(2,128)(2,1)} %bitcast.128) | data formatting | bytes 4194304 | tf_op jit(solution)/shard_map/all_to_all | solution.py:104
  254.1 2.7 fusion.59
  256.9 3.2 fusion.8
  262.4 1.4 copy-done.8
  264.7 3.5 copy.117
  268.3 4.6 all-to-all-start.4
  275.4 3.6 copy.114
  279.0 19.6 %all-to-all-done.4 = bf16[2,128,4096]{2,0,1:T(2,128)(2,1)} async-done(((bf16[2,128,4096]{2,0,1:T(2,128)(2,1)}), bf16[2,128,4096]{2,0,1:T(2,128)(2,1)}, u32[]{:S(2)}, u32[]{:S(2)}) %all-to-all-start.4) | async-done | bytes 2097184 | tf_op jit(solution)/shard_map/all_to_all | solution.py:121
  298.6 4.9 %all-to-all-start.3 = ((bf16[2,128,4096]{2,0,1:T(2,128)(2,1)}), bf16[2,128,4096]{2,0,1:T(2,128)(2,1)}, u32[]{:S(2)}, u32[]{:S(2)}) async-start(bf16[2,128,4096]{2,0,1:T(2,128)(2,1)} %copy.114), calls=%async_computation.3 | async-start | bytes 4194304 | tf_op jit(solution)/shard_map/all_to_all | solution.py:120
  304.8 4.8 %copy.157 = bf16[2,4,32,4096]{3,1,2,0:T(4,128)(2,1)} copy(bf16[2,4,32,4096]{3,0,2,1:T(2,128)(2,1)} %bitcast.39) | data formatting | bytes 4194304 | tf_op jit(solution)/shard_map/all_to_all | solution.py:121
  309.7 3.8 reshape.63
  313.4 3.1 fusion.45
  316.6 12.6 %all-to-all-done.3 = bf16[2,128,4096]{2,0,1:T(2,128)(2,1)} async-done(((bf16[2,128,4096]{2,0,1:T(2,128)(2,1)}), bf16[2,128,4096]{2,0,1:T(2,128)(2,1)}, u32[]{:S(2)}, u32[]{:S(2)}) %all-to-all-start.3) | async-done | bytes 2097184 | tf_op jit(solution)/shard_map/all_to_all | solution.py:120
  329.2 4.9 %copy.158 = bf16[2,4,32,4096]{3,1,2,0:T(4,128)(2,1)} copy(bf16[2,4,32,4096]{3,0,2,1:T(2,128)(2,1)} %bitcast.34) | data formatting | bytes 4194304 | tf_op jit(solution)/shard_map/all_to_all | solution.py:120
  334.0 4.8 %reshape.62 = bf16[2,32,128,128]{3,2,1,0:T(8,128)(2,1)} reshape(bf16[2,32,4,4096]{3,2,1,0:T(4,128)(2,1)} %bitcast.138) | data formatting | bytes 4194304 | tf_op jit(solution)/shard_map/reshape | solution.py:122
  338.8 2.9 fusion.47
  342.3 1.1 fusion.34
  343.4 1.2 fusion.33
  345.0 4.8 %select_reduce_fusion.1 = (bf16[32,128,128]{2,1,0:T(8,128)(2,1)S(1)}, bf16[32,128,128]{2,1,0:T(8,128)(2,1)S(1)}, f32[2,32,128,128]{3,2,1,0:T(8,128)}) fusion(bf16[2,32,128,128]{3,2,1,0:T(8,128)(2,1)S(1)} %copy-done.12, f32[2]{0:T(128)S(1)} %compare_select_fusion.5, pred[2]{0:T(512)(128)(4,1)S(1)} %get-tuple-element.19, ...), kind=kOutput, calls=%fused_computation.38 | convolution fusion | flops 551682048 | bytes 12648460 | tf_op jit(solution)/shard_map/pxyk,zk->pxyz/dot_general | solution.py:33
  350.0 1.4 copy.123
  351.4 51.4 %all_to_all.81 = bf16[2,32,128,128]{3,1,0,2:T(8,128)(2,1)S(1)} all-to-all(bf16[2,32,128,128]{3,1,0,2:T(8,128)(2,1)S(1)} %copy.123), channel_id=1, replica_groups=mesh['band'=8,'grid'=4] {'band'}, dimensions={2} | all-to-all | bytes 4194304 | tf_op jit(solution)/shard_map/all_to_all | solution.py:47
  402.8 1.4 copy.124
  404.2 2.3 gather_fusion.5
  406.5 2.2 copy.125
  409.4 2.7 copy.126
  412.1 4.5 all-to-all-start.6
  417.2 46.7 %all-to-all-done.6 = bf16[2,32,128,128]{3,1,0,2:T(8,128)(2,1)} async-done(((bf16[2,32,128,128]{3,1,0,2:T(8,128)(2,1)}), bf16[2,32,128,128]{3,1,0,2:T(8,128)(2,1)}, u32[]{:S(2)}, u32[]{:S(2)}) %all-to-all-start.6) | async-done | bytes 2097184 | tf_op jit(solution)/shard_map/all_to_all | solution.py:53
  463.9 6.7 %fusion.12 = f32[2,32,128,128]{3,2,1,0:T(8,128)} fusion(f32[2,32,128,128]{3,2,1,0:T(8,128)} %get-tuple-element.17, bf16[2,32,128,128]{3,1,0,2:T(8,128)(2,1)} %all-to-all-done.6, f32[2]{0:T(128)S(1)} %broadcast_select_fusion.2, bf16[2,32,128,128]{3,2,1,0:T(8,128)(2,1)S(1)} %copy-done.4, pred[2]{0:T(512)(128)(4,1)S(1)} %compare_and_fusion.1), kind=kLoop, calls=%fused_computation.26 | loop fusion | flops 7340032 | bytes 12582922 | tf_op jit(solution)/shard_map/neg | solution.py:149
  (76 shorter events, 18.1 us)
Async XLA Ops:
  2.5 10.7 %copy-start.15 = (s32[8]{0:T(128)S(1)}, s32[8]{0:T(128)}, u32[]{:S(2)}) copy-start(s32[8]{0:T(128)} %param.13) | copy-start | bytes 100
  3.7 13.1 %collective-permute-start = (bf16[2,32,16,128]{3,2,1,0:T(8,128)(2,1)}, bf16[2,32,16,128]{3,2,1,0:T(8,128)(2,1)}, u32[]{:S(2)}, u32[]{:S(2)}) collective-permute-start(bf16[2,32,16,128]{3,2,1,0:T(8,128)(2,1)} %get-tuple-element.14), channel_id=1, source_target_pairs={{0,28},{4,0},{8,4},{12,8},{16,12},{20,16},{24,20},{28,24},{1,29},{... | collective-permute-start | bytes 786440 | tf_op jit(solution)/shard_map/ppermute | solution.py:20
  9.7 12.7 %collective-permute-start.1 = (bf16[2,32,16,128]{3,2,1,0:T(8,128)(2,1)}, bf16[2,32,16,128]{3,2,1,0:T(8,128)(2,1)}, u32[]{:S(2)}, u32[]{:S(2)}) collective-permute-start(bf16[2,32,16,128]{3,2,1,0:T(8,128)(2,1)} %get-tuple-element.13), channel_id=1, source_target_pairs={{0,24},{4,28},{8,0},{12,4},{16,8},{20,12},{24,16},{28,20},{1,25},{... | collective-permute-start | bytes 786440 | tf_op jit(solution)/shard_map/ppermute | solution.py:20
  10.2 17.9 %collective-permute-start.2 = (bf16[2,32,16,128]{3,2,1,0:T(8,128)(2,1)S(1)}, bf16[2,32,16,128]{3,2,1,0:T(8,128)(2,1)}, u32[]{:S(2)}, u32[]{:S(2)}) collective-permute-start(bf16[2,32,16,128]{3,2,1,0:T(8,128)(2,1)S(1)} %get-tuple-element.12), channel_id=1, source_target_pairs={{0,20},{4,24},{8,28},{12,0},{16,4},{20,8},{24,12},{28,16},{1,21},{... | collective-permute-start | bytes 786440 | tf_op jit(solution)/shard_map/ppermute | solution.py:20
  10.2 44.6 %collective-permute-start.3 = (bf16[2,32,16,128]{3,2,1,0:T(8,128)(2,1)S(1)}, bf16[2,32,16,128]{3,2,1,0:T(8,128)(2,1)}, u32[]{:S(2)}, u32[]{:S(2)}) collective-permute-start(bf16[2,32,16,128]{3,2,1,0:T(8,128)(2,1)S(1)} %get-tuple-element.11), channel_id=1, source_target_pairs={{0,16},{4,20},{8,24},{12,28},{16,0},{20,4},{24,8},{28,12},{1,17},{... | collective-permute-start | bytes 786440 | tf_op jit(solution)/shard_map/ppermute | solution.py:20
  13.2 42.6 %collective-permute-start.4 = (bf16[2,32,16,128]{3,2,1,0:T(8,128)(2,1)S(1)}, bf16[2,32,16,128]{3,2,1,0:T(8,128)(2,1)}, u32[]{:S(2)}, u32[]{:S(2)}) collective-permute-start(bf16[2,32,16,128]{3,2,1,0:T(8,128)(2,1)S(1)} %get-tuple-element.10), channel_id=1, source_target_pairs={{0,12},{4,16},{8,20},{12,24},{16,28},{20,0},{24,4},{28,8},{1,13},{... | collective-permute-start | bytes 786440 | tf_op jit(solution)/shard_map/ppermute | solution.py:20
  16.8 39.9 %collective-permute-start.5 = (bf16[2,32,16,128]{3,2,1,0:T(8,128)(2,1)S(1)}, bf16[2,32,16,128]{3,2,1,0:T(8,128)(2,1)S(1)}, u32[]{:S(2)}, u32[]{:S(2)}) collective-permute-start(bf16[2,32,16,128]{3,2,1,0:T(8,128)(2,1)S(1)} %get-tuple-element.9), channel_id=1, source_target_pairs={{0,8},{4,12},{8,16},{12,20},{16,24},{20,28},{24,0},{28,4},{1,9},{5... | collective-permute-start | bytes 786440 | tf_op jit(solution)/shard_map/ppermute | solution.py:20
  22.4 34.4 %collective-permute-start.6 = (bf16[2,32,16,128]{3,2,1,0:T(8,128)(2,1)S(1)}, bf16[2,32,16,128]{3,2,1,0:T(8,128)(2,1)S(1)}, u32[]{:S(2)}, u32[]{:S(2)}) collective-permute-start(bf16[2,32,16,128]{3,2,1,0:T(8,128)(2,1)S(1)} %get-tuple-element.8), channel_id=1, source_target_pairs={{0,4},{4,8},{8,12},{12,16},{16,20},{20,24},{24,28},{28,0},{1,5},{5... | collective-permute-start | bytes 786440 | tf_op jit(solution)/shard_map/ppermute | solution.py:20
  65.6 6.3 %copy-start.13 = (bf16[2,32,128,128]{3,2,1,0:T(8,128)(2,1)S(1)}, bf16[2,32,128,128]{3,2,1,0:T(8,128)(2,1)}, u32[]{:S(2)}) copy-start(bf16[2,32,128,128]{3,2,1,0:T(8,128)(2,1)} %param.11) | copy-start | bytes 6291460
  65.6 52.7 %all-to-all-start = ((bf16[2,32,128,128]{3,1,0,2:T(8,128)(2,1)}), bf16[2,32,128,128]{3,1,0,2:T(8,128)(2,1)}, u32[]{:S(2)}, u32[]{:S(2)}) async-start(bf16[2,32,128,128]{3,1,0,2:T(8,128)(2,1)} %copy.98), calls=%async_computation | async-start | bytes 4194304 | tf_op jit(solution)/shard_map/all_to_all | solution.py:42
  125.1 3.7 copy-start.3
  128.7 2.0 copy-start
  151.7 33.2 %all-to-all-start.2 = ((bf16[4,2,131072]{2,1,0:T(2,128)(2,1)}), bf16[4,2,131072]{2,1,0:T(2,128)(2,1)S(1)}, u32[]{:S(2)}, u32[]{:S(2)}) async-start(bf16[4,2,131072]{2,1,0:T(2,128)(2,1)} %reshape.144), calls=%async_computation.2 | async-start | bytes 4194304 | tf_op jit(solution)/shard_map/all_to_all | solution.py:105
  155.5 2.8 copy-start.1
  185.0 43.7 %all-to-all-start.1 = ((bf16[4,2,131072]{2,1,0:T(2,128)(2,1)}), bf16[4,2,131072]{2,1,0:T(2,128)(2,1)}, u32[]{:S(2)}, u32[]{:S(2)}) async-start(bf16[4,2,131072]{2,1,0:T(2,128)(2,1)} %reshape.146), calls=%async_computation.1 | async-start | bytes 4194304 | tf_op jit(solution)/shard_map/all_to_all | solution.py:104
  254.1 2.7 copy-start.2
  254.1 2.9 copy-start.5
  260.1 1.3 copy-start.6
  262.4 1.4 copy-start.8
  268.3 4.6 copy-start.9
  268.3 30.3 %all-to-all-start.4 = ((bf16[2,128,4096]{2,0,1:T(2,128)(2,1)}), bf16[2,128,4096]{2,0,1:T(2,128)(2,1)}, u32[]{:S(2)}, u32[]{:S(2)}) async-start(bf16[2,128,4096]{2,0,1:T(2,128)(2,1)} %copy.117), calls=%async_computation.4 | async-start | bytes 4194304 | tf_op jit(solution)/shard_map/all_to_all | solution.py:121
  272.9 1.6 copy-start.7
  278.9 25.1 %copy-start.14 = (f32[16]{0:T(128)S(1)}, f32[16]{0:T(128)}, u32[]{:S(2)}) copy-start(f32[16]{0:T(128)} %param.12) | copy-start | bytes 196
  298.6 30.6 %all-to-all-start.3 = ((bf16[2,128,4096]{2,0,1:T(2,128)(2,1)}), bf16[2,128,4096]{2,0,1:T(2,128)(2,1)}, u32[]{:S(2)}, u32[]{:S(2)}) async-start(bf16[2,128,4096]{2,0,1:T(2,128)(2,1)} %copy.114), calls=%async_computation.3 | async-start | bytes 4194304 | tf_op jit(solution)/shard_map/all_to_all | solution.py:120
  338.8 2.9 copy-start.10
  338.8 3.5 copy-start.11
  343.4 1.6 copy-start.12
  412.1 51.8 %copy-start.4 = (bf16[2,32,128,128]{3,2,1,0:T(8,128)(2,1)S(1)}, bf16[2,32,128,128]{3,2,1,0:T(8,128)(2,1)}, u32[]{:S(2)}) copy-start(bf16[2,32,128,128]{3,2,1,0:T(8,128)(2,1)} %copy-done.3) | copy-start | bytes 6291460
  412.1 51.8 %all-to-all-start.6 = ((bf16[2,32,128,128]{3,1,0,2:T(8,128)(2,1)}), bf16[2,32,128,128]{3,1,0,2:T(8,128)(2,1)}, u32[]{:S(2)}, u32[]{:S(2)}) async-start(bf16[2,32,128,128]{3,1,0,2:T(8,128)(2,1)} %copy.126), calls=%async_computation.6 | async-start | bytes 4194304 | tf_op jit(solution)/shard_map/all_to_all | solution.py:53
